TPU v7x, 32 devices: a whole 2x2x4 slice. The times are simulated.
32 devices in a mesh: dp: 8 (over z, core), sp: 4 (over y, x).
Axes of the slice: x: 2, y: 2, z: 4, core: 2. Of those that a mesh axis runs over, the one named last changes fastest.
Arguments:
- gate_pre: bfloat16 [2048, 8192], P('dp', 'sp'), may hold values from -6 to 6
- up_pre: bfloat16 [2048, 8192], P('dp', 'sp'), may hold values from -6 to 6
- w_down: bfloat16 [8192, 6144], P('sp'), may hold values from -0.0625 to 0.0625
- route_logits: float32 [4096, 2], P(('dp', 'sp')), may hold values from -8 to 8
- expert_ids: int32 [4096, 2], P(('dp', 'sp')), may hold values from 0 to 7, as said below
- d_out: bfloat16 [4096, 6144], P(('dp', 'sp')), may hold values from -6 to 6
Outputs:
- mixed: bfloat16 [4096, 6144], P(('dp', 'sp'))
- logit_grads: float32 [4096, 2], P(('dp', 'sp'))
- gate_grads: bfloat16 [2048, 8192], P('dp', 'sp')
- up_grads: bfloat16 [2048, 8192], P('dp', 'sp')
- down_grads: float32 [8192, 6144], P('sp', 'dp')
Inputs may be any that keep to these rules, and one draw needn't show every extreme that they name: `expert_ids`: each row names two different experts. Of the 128 rows of one device, a quarter of 64 up to 64 name expert 0, and exactly 64 on some device in every draw.
All inputs are finite; a program needn't handle non-finite values.
Results may differ from a plain program's by a relative error of at most 0.022.
Values may be sent and summed in bfloat16 or wider, within the bound.
A program may use at most 128 MiB of HBM per device.

v0:
```python
import jax
import jax.numpy as jnp
from jax import lax
from jax.sharding import PartitionSpec as P


def contract_rows(left, right):
    return lax.dot_general(
        left, right, (((0,), (0,)), ((), ())), preferred_element_type=jnp.float32
    )


def contract_cols(left, right):
    return lax.dot_general(
        left, right, (((1,), (1,)), ((), ())), preferred_element_type=jnp.float32
    )


def plain_product(left, right):
    return jnp.dot(left, right, preferred_element_type=jnp.float32)


def local(gate_pre, up_pre, w_down, route_logits, expert_ids, d_out):
    tok_rows = expert_ids.shape[0]
    slot_rows = tok_rows // 2
    routed = jnp.any(expert_ids == 0, axis=1)
    routed_int = routed.astype(jnp.int32)
    routed_float = routed.astype(jnp.float32)
    slot_rank = jnp.cumsum(routed_int) - 1
    gate_wide = gate_pre.astype(jnp.float32)
    up_wide = up_pre.astype(jnp.float32)
    sigma_gate = jax.nn.sigmoid(gate_wide)
    silu_gate = gate_wide * sigma_gate
    hidden = (silu_gate * up_wide).astype(jnp.bfloat16)
    expert_out = lax.psum_scatter(
        plain_product(hidden, w_down).astype(jnp.bfloat16), "sp", scatter_dimension=0, tiled=True
    ).astype(jnp.float32)
    safe_rank = jnp.clip(slot_rank, 0, slot_rows - 1)
    token_out = expert_out[safe_rank] * routed_float[:, None]
    first_zero = expert_ids[:, 0] == 0
    own_logit = jnp.where(first_zero, route_logits[:, 0], route_logits[:, 1])
    other_logit = jnp.where(first_zero, route_logits[:, 1], route_logits[:, 0])
    weight_zero = routed_float * jax.nn.sigmoid(own_logit - other_logit)
    mixed = (weight_zero[:, None] * token_out).astype(jnp.bfloat16)
    weight_grad = jnp.sum(d_out.astype(jnp.float32) * token_out, axis=1)
    logit_grad = weight_grad * weight_zero * (1.0 - weight_zero)
    first_col = jnp.where(first_zero, logit_grad, -logit_grad)
    logit_grads = jnp.stack([first_col, -first_col], axis=1)
    chooser = (slot_rank[:, None] == jnp.arange(slot_rows, dtype=jnp.int32)[None, :]) & routed[
        :, None
    ]
    picked = contract_rows(chooser.astype(jnp.bfloat16), d_out)
    slot_weight = lax.dot_general(
        chooser.astype(jnp.float32),
        weight_zero,
        (((0,), (0,)), ((), ())),
        precision=lax.Precision.HIGHEST,
        preferred_element_type=jnp.float32,
    )
    d_expert = (slot_weight[:, None] * picked).astype(jnp.bfloat16)
    piece = lax.all_gather(d_expert, "sp", axis=0, tiled=True)
    part_hidden = contract_cols(piece, w_down)
    d_hidden = part_hidden
    extra_part = piece
    d_hidden, extra_part = (d_hidden, extra_part)
    cycle_blocks = lax.all_to_all(extra_part, "dp", split_axis=1, concat_axis=0, tiled=True)
    down_grads = contract_rows(lax.all_gather(hidden, "dp", axis=0, tiled=True), cycle_blocks)
    gate_grads = (d_hidden * up_wide * sigma_gate * (1.0 + gate_wide * (1.0 - sigma_gate))).astype(
        jnp.bfloat16
    )
    up_grads = (d_hidden * silu_gate).astype(jnp.bfloat16)
    return (mixed, logit_grads, gate_grads, up_grads, down_grads)


def solution(mesh):
    return jax.shard_map(
        local,
        mesh=mesh,
        in_specs=(
            P("dp", "sp"),
            P("dp", "sp"),
            P("sp", None),
            P(("dp", "sp"), None),
            P(("dp", "sp"), None),
            P(("dp", "sp"), None),
        ),
        out_specs=(
            P(("dp", "sp"), None),
            P(("dp", "sp"), None),
            P("dp", "sp"),
            P("dp", "sp"),
            P("sp", "dp"),
        ),
        check_vma=False,
    )
```

profile of v0, /device:TPU:0, one launch (start us, length us, event | category | flops | bytes accessed | tf_op | source)
XLA Modules:
  0.0 289.5 jit_solution(3769832607676820949)
XLA Ops:
  7.2 0.0 reduce-scatter.2.cloned.1.call-start
  7.2 2.2 fusion.1
  9.4 0.0 copy-start.2
  9.4 13.1 %convolution_convert_fusion = bf16[256,6144]{1,0:T(8,128)(2,1)} fusion(bf16[256,2048]{1,0:T(8,128)(2,1)S(1)} %fusion.1, bf16[2048,6144]{1,0:T(8,128)(2,1)} %param.8), kind=kOutput, calls=%fused_computation.1 | convolution fusion | flops 6444023808 | bytes 29360128 | tf_op jit(solution)/shard_map/dot_general | solution.py:20
  22.5 0.0 copy-done.2
  22.5 0.0 copy-start.4
  22.5 0.0 reduce-scatter.2.cloned.1.call-update
  22.6 0.0 all-gather.3.cloned.1.call-start
  22.6 0.6 copy-done.4
  23.3 0.1 copy.50
  23.4 0.2 reduce-window.4
  23.5 0.1 copy.51
  23.6 45.7 %reduce-scatter.2.cloned.1.call-done = bf16[64,6144]{1,0:T(8,128)(2,1)} async-done(((bf16[256,6144]{1,0:T(8,128)(2,1)}), bf16[64,6144]{1,0:T(8,128)(2,1)}) %reduce-scatter.2.cloned.1.call-update) | async-done | bytes 786448 | tf_op jit(solution)/shard_map/reduce_scatter | solution.py:35
  69.3 1.2 convert_element_type.53
  70.6 0.0 copy-start.1
  70.6 3.2 %gather_fusion = f32[128,6144]{1,0:T(8,128)} fusion(f32[64,6144]{1,0:T(8,128)S(1)} %convert_element_type.53, s32[1024]{0:T(1024)S(1)} %pad_clamp_fusion), kind=kCustom, calls=%fused_computation | custom fusion | bytes 6291968 | tf_op jit(solution)/shard_map/gather | solution.py:39
  73.8 0.0 copy-start.3
  73.8 0.0 copy-done.1
  73.8 2.5 multiply_reduce_fusion
  76.3 0.0 copy-done.3
  76.3 0.2 convolution_bitcast_fusion
  76.5 1.4 fusion
  77.9 0.0 all-gather.3.cloned.1.call-update
  77.9 0.0 all-gather.5.cloned.1.call-start
  78.0 0.7 all-gather.5.cloned.1.call-update
  78.7 43.3 %all-gather.3.cloned.1.call-done = bf16[256,6144]{1,0:T(8,128)(2,1)} async-done(((bf16[64,6144]{1,0:T(8,128)(2,1)}), bf16[256,6144]{1,0:T(8,128)(2,1)}) %all-gather.3.cloned.1.call-update) | async-done | bytes 3145744 | tf_op jit(solution)/shard_map/all_gather | solution.py:61
  121.9 3.7 %copy.55 = bf16[32,8,8,768]{3,2,0,1:T(8,128)(2,1)} copy(bf16[32,8,8,768]{3,2,1,0:T(8,128)(2,1)} %bitcast.46) | data formatting | bytes 6291456 | tf_op jit(solution)/shard_map/all_to_all | solution.py:66
  125.6 0.0 copy-start
  125.6 4.9 %all-to-all-start = ((bf16[256,8,768]{2,0,1:T(8,128)(2,1)}), bf16[256,8,768]{2,0,1:T(8,128)(2,1)}, u32[]{:S(2)}, u32[]{:S(2)}) async-start(bf16[256,8,768]{2,0,1:T(8,128)(2,1)} %bitcast.45), calls=%async_computation.1 | async-start | bytes 6291456 | tf_op jit(solution)/shard_map/all_to_all | solution.py:66
  130.6 0.6 pad_maximum_fusion
  131.1 0.0 copy-done
  131.1 1.6 multiply_convert_fusion
  132.7 14.7 %multiply_convert_fusion.1 = (bf16[256,2048]{1,0:T(8,128)(2,1)}, bf16[256,2048]{1,0:T(8,128)(2,1)}) fusion(bf16[256,2048]{1,0:T(8,128)(2,1)} %param.6, bf16[256,2048]{1,0:T(8,128)(2,1)} %param.7, bf16[256,6144]{1,0:T(8,128)(2,1)} %all-gather.3.cloned.1.call-done, bf16[2048,6144]{1,0:T(8,128)(2,1)} %param.8), kind=kOutput, calls=%fused_computation.20 | convolution fusion | flops 6450315264 | bytes 32505856 | tf_op jit(solution)/shard_map/dot_general | solution.py:14
  147.4 123.7 %all-gather.5.cloned.1.call-done = bf16[2048,2048]{1,0:T(8,128)(2,1)} async-done(((bf16[256,2048]{1,0:T(8,128)(2,1)}), bf16[2048,2048]{1,0:T(8,128)(2,1)}) %all-gather.5.cloned.1.call-update) | async-done | bytes 8388624 | tf_op jit(solution)/shard_map/all_gather | solution.py:67
  271.1 0.0 all-to-all-done
  271.1 11.9 %fusion.24 = f32[2048,768]{1,0:T(8,128)} fusion(bf16[2048,2048]{1,0:T(8,128)(2,1)} %all-gather.5.cloned.1.call-done, bf16[2048,768]{1,0:T(8,128)(2,1)} %bitcast.9), kind=kOutput, calls=%fused_computation.47 | convolution fusion | flops 6442450944 | bytes 17825792 | tf_op jit(solution)/shard_map/dot_general | solution.py:8
  (6 shorter events, 0.1 us)
Async XLA Ops:
  7.2 62.2 %reduce-scatter.2.cloned.1.call-start = ((), (), s32[]{:S(2)}) async-start(), calls=%async_computation.2 | async-start | bytes 3932160 | tf_op jit(solution)/shard_map/reduce_scatter | solution.py:35
  9.4 13.1 %copy-start.2 = (bf16[256,2048]{1,0:T(8,128)(2,1)}, bf16[256,2048]{1,0:T(8,128)(2,1)S(1)}, u32[]{:S(2)}) copy-start(bf16[256,2048]{1,0:T(8,128)(2,1)S(1)} %fusion.1) | copy-start | bytes 3145732
  22.5 0.7 copy-start.4
  22.6 99.4 %all-gather.3.cloned.1.call-start = ((), (), s32[]{:S(2)}) async-start(), calls=%async_computation.3 | async-start | bytes 3932160 | tf_op jit(solution)/shard_map/all_gather | solution.py:61
  70.6 3.2 %copy-start.1 = (bf16[128,6144]{1,0:T(8,128)(2,1)S(1)}, bf16[128,6144]{1,0:T(8,128)(2,1)}, u32[]{:S(2)}) copy-start(bf16[128,6144]{1,0:T(8,128)(2,1)} %param.11) | copy-start | bytes 4718596
  73.8 2.5 copy-start.3
  77.9 193.2 %all-gather.5.cloned.1.call-start = ((), (), s32[]{:S(2)}) async-start(), calls=%async_computation.4 | async-start | bytes 9437184 | tf_op jit(solution)/shard_map/all_gather | solution.py:67
  125.6 5.5 %copy-start = (f32[128,6144]{1,0:T(8,128)S(1)}, f32[128,6144]{1,0:T(8,128)}, u32[]{:S(2)}) copy-start(f32[128,6144]{1,0:T(8,128)} %gather_fusion) | copy-start | bytes 9437188
  125.6 145.4 %all-to-all-start = ((bf16[256,8,768]{2,0,1:T(8,128)(2,1)}), bf16[256,8,768]{2,0,1:T(8,128)(2,1)}, u32[]{:S(2)}, u32[]{:S(2)}) async-start(bf16[256,8,768]{2,0,1:T(8,128)(2,1)} %bitcast.45), calls=%async_computation.1 | async-start | bytes 6291456 | tf_op jit(solution)/shard_map/all_to_all | solution.py:66
Sparse Core Ops, SparseCore 0:
  22.7 46.6 reduce-scatter.1
  78.0 43.8 all-gather.2
  123.5 147.4 all-gather.4
where the time goes:
time: 290 us; the launch traced here: 289 us
  waiting for transfers between devices  213 us (73%)
  matrix products  41.3 us (14%)
  between operations  13.8 us (5%)
  other arithmetic  8.3 us (3%)
  local copies, waits for them, and re-layouts  7.69 us (3%)
  starting transfers between devices  5.04 us (2%)
    all_gather x1, waiting for transfers between devices, local(): lax.all_gather(hidden, 'dp', axis=0, tiled=True)  124 us
    reduce_scatter x1, waiting for transfers between devices, local(): lax.psum_scatter(plain_product(hidden, w_down).astype(jnp.bfloat16), 'sp'...  45.7 us
    all_gather x1, waiting for transfers between devices, local(): piece = lax.all_gather(d_expert, 'sp', axis=0, tiled=True)  43.3 us
    dot_general x1, matrix products, contract_cols(): lax.dot_general(left, right, (((1,), (1,)), ((), ())), preferred_element_...  14.7 us
    dot_general x2, matrix products, contract_rows(): lax.dot_general(left, right, (((0,), (0,)), ((), ())), preferred_element_...  13.3 us
    dot_general x1, matrix products, plain_product(): return jnp.dot(left, right, preferred_element_type=jnp.float32)  13.1 us
  transfers between devices with their start and end apart: 4, of which 3 were waited for; matrix products, arithmetic and copies ran while one was open for 7% of the time, Pallas kernels for 0%

commit v1 on v0

--- a/solution.py
+++ b/solution.py
@@ -58,7 +58,12 @@
         preferred_element_type=jnp.float32,
     )
     d_expert = (slot_weight[:, None] * picked).astype(jnp.bfloat16)
-    piece = lax.all_gather(d_expert, "sp", axis=0, tiled=True)
+    ring = [d_expert]
+    for hop in range(3):
+        ring.append(lax.ppermute(ring[-1], "sp", [(dev, (dev + 1) % 4) for dev in range(4)]))
+    piece = jnp.roll(
+        jnp.concatenate(ring[::-1], axis=0), (lax.axis_index("sp") + 1) * ring[0].shape[0], axis=0
+    )
     part_hidden = contract_cols(piece, w_down)
     d_hidden = part_hidden
     extra_part = piece

time: 290 us -> 238 us (0.82)
  waiting for transfers between devices: 213 us -> 157 us
    all_gather x1, waiting for transfers between devices: 124 us -> 0.03 us  [local(): lax.all_gather(hidden, 'dp', axis=0, tiled=True)]
    ppermute x0 -> x3, waiting for transfers between devices: none -> 55.8 us  [local(): lax.ppermute(ring[-1], 'sp', [(dev, (dev + 1) % 4) for dev in range(4)])]
    all_to_all x1, waiting for transfers between devices: 0.01 us -> 54.9 us  [local(): lax.all_to_all(extra_part, 'dp', split_axis=1, concat_axis=0, tiled=True)]
    all_gather x1 -> x0, waiting for transfers between devices: 43.3 us -> none  [local(): piece = lax.all_gather(d_expert, 'sp', axis=0, tiled=True)]
    dynamic_slice x0 -> x2, local copies, waits for them, and re-layouts: none -> 3.45 us  [local(): jnp.roll(jnp.concatenate(ring[::-1], axis=0), (lax.axis_index('sp') + 1)...]
  transfers between devices with their start and end apart: 4 -> 6, of which waited for: 3 -> 5; matrix products, arithmetic and copies ran while one was open for 7% -> 13% of each run, Pallas kernels for 0% -> 0%
where the time goes in v1:
time: 238 us
  waiting for transfers between devices  157 us (66%)
  matrix products  39.2 us (16%)
  between operations  15.6 us (7%)
  local copies, waits for them, and re-layouts  10.5 us (4%)
  other arithmetic  8.33 us (4%)
  starting transfers between devices  7.11 us (3%)
    ppermute x3, waiting for transfers between devices, local(): lax.ppermute(ring[-1], 'sp', [(dev, (dev + 1) % 4) for dev in range(4)])  55.8 us
    all_to_all x1, waiting for transfers between devices, local(): lax.all_to_all(extra_part, 'dp', split_axis=1, concat_axis=0, tiled=True)  54.9 us
    reduce_scatter x1, waiting for transfers between devices, local(): lax.psum_scatter(plain_product(hidden, w_down).astype(jnp.bfloat16), 'sp'...  45.7 us
    dot_general x1, matrix products, contract_cols(): lax.dot_general(left, right, (((1,), (1,)), ((), ())), preferred_element_...  14.5 us
    dot_general x1, matrix products, plain_product(): return jnp.dot(left, right, preferred_element_type=jnp.float32)  13.1 us
    dot_general x2, matrix products, contract_rows(): lax.dot_general(left, right, (((0,), (0,)), ((), ())), preferred_element_...  11.4 us
    all_to_all x1, starting transfers between devices, local(): lax.all_to_all(extra_part, 'dp', split_axis=1, concat_axis=0, tiled=True)  4.93 us
  transfers between devices with their start and end apart: 6, of which 5 were waited for; matrix products, arithmetic and copies ran while one was open for 13% of the time, Pallas kernels for 0%

profile of v1, /device:TPU:0, one launch (start us, length us, event | category | flops | bytes accessed | tf_op | source)
XLA Modules:
  0.0 237.8 jit_solution(6880707699554246688)
XLA Ops:
  8.0 0.0 reduce-scatter.2.cloned.1.call-start
  8.0 2.2 fusion.1
  10.3 0.0 copy-start.3
  10.3 13.1 %convolution_convert_fusion = bf16[256,6144]{1,0:T(8,128)(2,1)} fusion(bf16[256,2048]{1,0:T(8,128)(2,1)S(1)} %fusion.1, bf16[2048,6144]{1,0:T(8,128)(2,1)} %param.8), kind=kOutput, calls=%fused_computation.1 | convolution fusion | flops 6444023808 | bytes 29360128 | tf_op jit(solution)/shard_map/dot_general | solution.py:20
  23.4 0.0 copy-done.3
  23.4 0.0 reduce-scatter.2.cloned.1.call-update
  23.4 0.0 all-gather.2.cloned.1.call-start
  23.5 0.5 all-gather.2.cloned.1.call-update
  24.0 0.1 copy-done.5
  24.1 0.1 copy.64
  24.2 0.2 reduce-window.4
  24.4 0.1 copy.65
  24.5 45.7 %reduce-scatter.2.cloned.1.call-done = bf16[64,6144]{1,0:T(8,128)(2,1)} async-done(((bf16[256,6144]{1,0:T(8,128)(2,1)}), bf16[64,6144]{1,0:T(8,128)(2,1)}) %reduce-scatter.2.cloned.1.call-update) | async-done | bytes 786448 | tf_op jit(solution)/shard_map/reduce_scatter | solution.py:35
  70.2 1.3 convert_element_type.53
  71.4 0.0 copy-start.2
  71.5 3.2 %gather_fusion = f32[128,6144]{1,0:T(8,128)} fusion(f32[64,6144]{1,0:T(8,128)S(1)} %convert_element_type.53, s32[1024]{0:T(1024)S(1)} %pad_clamp_fusion), kind=kCustom, calls=%fused_computation | custom fusion | bytes 6291968 | tf_op jit(solution)/shard_map/gather | solution.py:39
  74.6 0.0 copy-done.2
  74.6 2.5 %multiply_reduce_fusion = f32[128]{0:T(128)S(1)} fusion(bf16[128,6144]{1,0:T(8,128)(2,1)S(1)} %copy-done.2, f32[128,6144]{1,0:T(8,128)} %gather_fusion, f32[128]{0:T(128)S(1)} %get-tuple-element.27), kind=kLoop, calls=%fused_computation.4 | loop fusion | flops 3145600 | bytes 4719616 | tf_op jit(solution)/shard_map/reduce_sum | solution.py:45
  77.1 0.0 copy-done.4
  77.1 0.2 convolution_bitcast_fusion
  77.4 0.5 fusion
  77.9 1.5 collective-permute-start
  79.4 18.6 %collective-permute-done = bf16[64,6144]{1,0:T(8,128)(2,1)S(1)} collective-permute-done((bf16[64,6144]{1,0:T(8,128)(2,1)S(1)}, bf16[64,6144]{1,0:T(8,128)(2,1)S(1)}, u32[]{:S(2)}, u32[]{:S(2)}) %collective-permute-start) | collective-permute-done | bytes 786464 | tf_op jit(solution)/shard_map/ppermute | solution.py:63
  98.0 0.6 collective-permute-start.1
  98.6 18.7 %collective-permute-done.1 = bf16[64,6144]{1,0:T(8,128)(2,1)S(1)} collective-permute-done((bf16[64,6144]{1,0:T(8,128)(2,1)S(1)}, bf16[64,6144]{1,0:T(8,128)(2,1)S(1)}, u32[]{:S(2)}, u32[]{:S(2)}) %collective-permute-start.1) | collective-permute-done | bytes 786464 | tf_op jit(solution)/shard_map/ppermute | solution.py:63
  117.3 0.0 collective-permute-start.2
  117.3 18.5 %collective-permute-done.2 = bf16[64,6144]{1,0:T(8,128)(2,1)S(1)} collective-permute-done((bf16[64,6144]{1,0:T(8,128)(2,1)S(1)}, bf16[64,6144]{1,0:T(8,128)(2,1)S(1)}, u32[]{:S(2)}, u32[]{:S(2)}) %collective-permute-start.2) | collective-permute-done | bytes 786464 | tf_op jit(solution)/shard_map/ppermute | solution.py:63
  135.8 0.1 constant_dynamic-update-slice_fusion.7
  135.8 0.1 constant_dynamic-update-slice_fusion.6
  135.9 0.1 constant_dynamic-update-slice_fusion.5
  135.9 0.1 constant_dynamic-update-slice_fusion.4
  136.0 0.1 constant_dynamic-update-slice_fusion.3
  136.1 0.1 constant_dynamic-update-slice_fusion.2
  136.1 0.1 constant_dynamic-update-slice_fusion.1
  136.2 0.1 constant_dynamic-update-slice_fusion
  136.3 0.2 constant_dynamic-slice_fusion
  136.5 0.0 copy-start.1
  136.5 3.2 %copy.66 = bf16[256,6144]{0,1:T(8,128)(2,1)} copy(bf16[256,6144]{1,0:T(8,128)(2,1)S(1)} %constant_dynamic-slice_fusion) | data formatting | bytes 6291456 | tf_op jit(solution)/shard_map/jit(_roll_dynamic)/dynamic_slice | solution.py:64
  139.7 0.0 copy-done.1
  139.7 4.9 %all-to-all-start = ((bf16[256,8,768]{0,2,1:T(8,128)(2,1)}), bf16[256,8,768]{0,2,1:T(8,128)(2,1)}, u32[]{:S(2)}, u32[]{:S(2)}) async-start(bf16[256,8,768]{0,2,1:T(8,128)(2,1)} %bitcast.41), calls=%async_computation.1 | async-start | bytes 6291456 | tf_op jit(solution)/shard_map/all_to_all | solution.py:71
  144.7 0.6 pad_maximum_fusion
  145.2 0.0 copy-done
  145.2 1.6 multiply_convert_fusion
  146.8 14.5 %multiply_convert_fusion.1 = (bf16[256,2048]{1,0:T(8,128)(2,1)}, bf16[256,2048]{1,0:T(8,128)(2,1)}) fusion(bf16[256,2048]{1,0:T(8,128)(2,1)} %param.6, bf16[256,2048]{1,0:T(8,128)(2,1)} %param.7, bf16[256,6144]{1,0:T(8,128)(2,1)} %copy-done.1, bf16[2048,6144]{1,0:T(8,128)(2,1)} %param.8), kind=kOutput, calls=%fused_computation.19 | convolution fusion | flops 6450315264 | bytes 32505856 | tf_op jit(solution)/shard_map/dot_general | solution.py:14
  161.3 54.9 %all-to-all-done = bf16[256,8,768]{0,2,1:T(8,128)(2,1)} async-done(((bf16[256,8,768]{0,2,1:T(8,128)(2,1)}), bf16[256,8,768]{0,2,1:T(8,128)(2,1)}, u32[]{:S(2)}, u32[]{:S(2)}) %all-to-all-start) | async-done | bytes 3145760 | tf_op jit(solution)/shard_map/all_to_all | solution.py:71
  216.2 3.2 %copy.67 = bf16[8,256,768]{2,1,0:T(8,128)(2,1)S(1)} copy(bf16[8,256,768]{1,2,0:T(8,128)(2,1)} %bitcast.9) | data formatting | bytes 6291456 | tf_op jit(solution)/shard_map/all_to_all | solution.py:71
  219.4 0.0 all-gather.2.cloned.1.call-done
  219.5 10.9 %fusion.24 = f32[2048,768]{1,0:T(8,128)} fusion(bf16[2048,2048]{1,0:T(8,128)(2,1)} %all-gather.2.cloned.1.call-done, bf16[2048,768]{1,0:T(8,128)(2,1)S(1)} %bitcast.42), kind=kOutput, calls=%fused_computation.55 | convolution fusion | flops 6442450944 | bytes 17825792 | tf_op jit(solution)/shard_map/dot_general | solution.py:8
  (9 shorter events, 0.1 us)
Async XLA Ops:
  8.0 62.2 %reduce-scatter.2.cloned.1.call-start = ((), (), s32[]{:S(2)}) async-start(), calls=%async_computation.2 | async-start | bytes 3932160 | tf_op jit(solution)/shard_map/reduce_scatter | solution.py:35
  10.3 13.1 %copy-start.3 = (bf16[256,2048]{1,0:T(8,128)(2,1)}, bf16[256,2048]{1,0:T(8,128)(2,1)S(1)}, u32[]{:S(2)}) copy-start(bf16[256,2048]{1,0:T(8,128)(2,1)S(1)} %fusion.1) | copy-start | bytes 3145732
  23.4 0.7 copy-start.5
  23.4 196.0 %all-gather.2.cloned.1.call-start = ((), (), s32[]{:S(2)}) async-start(), calls=%async_computation.3 | async-start | bytes 9437184 | tf_op jit(solution)/shard_map/all_gather | solution.py:72
  71.4 3.2 %copy-start.2 = (bf16[128,6144]{1,0:T(8,128)(2,1)S(1)}, bf16[128,6144]{1,0:T(8,128)(2,1)}, u32[]{:S(2)}) copy-start(bf16[128,6144]{1,0:T(8,128)(2,1)} %param.11) | copy-start | bytes 4718596
  74.6 2.5 %copy-start.4 = (f32[128,2]{0,1:T(2,128)S(1)}, f32[128,2]{0,1:T(2,128)}, u32[]{:S(2)}) copy-start(f32[128,2]{0,1:T(2,128)} %param.9) | copy-start | bytes 3076
  77.9 20.1 %collective-permute-start = (bf16[64,6144]{1,0:T(8,128)(2,1)S(1)}, bf16[64,6144]{1,0:T(8,128)(2,1)S(1)}, u32[]{:S(2)}, u32[]{:S(2)}) collective-permute-start(bf16[64,6144]{1,0:T(8,128)(2,1)S(1)} %fusion), channel_id=1, source_target_pairs={{0,1},{1,2},{2,3},{3,0},{4,5},{5,6},{6,7},{7,4},{8,9},{9,10},{10,1... | collective-permute-start | bytes 2359304 | tf_op jit(solution)/shard_map/ppermute | solution.py:63
  98.0 19.3 %collective-permute-start.1 = (bf16[64,6144]{1,0:T(8,128)(2,1)S(1)}, bf16[64,6144]{1,0:T(8,128)(2,1)S(1)}, u32[]{:S(2)}, u32[]{:S(2)}) collective-permute-start(bf16[64,6144]{1,0:T(8,128)(2,1)S(1)} %collective-permute-done), channel_id=1, source_target_pairs={{0,1},{1,2},{2,3},{3,0},{4,5},{5,6},{6,7},{7,4},{8,9},{9,10},{10,1... | collective-permute-start | bytes 2359304 | tf_op jit(solution)/shard_map/ppermute | solution.py:63
  117.3 18.5 %collective-permute-start.2 = (bf16[64,6144]{1,0:T(8,128)(2,1)S(1)}, bf16[64,6144]{1,0:T(8,128)(2,1)S(1)}, u32[]{:S(2)}, u32[]{:S(2)}) collective-permute-start(bf16[64,6144]{1,0:T(8,128)(2,1)S(1)} %collective-permute-done.1), channel_id=1, source_target_pairs={{0,1},{1,2},{2,3},{3,0},{4,5},{5,6},{6,7},{7,4},{8,9},{9,10},{10,1... | collective-permute-start | bytes 2359304 | tf_op jit(solution)/shard_map/ppermute | solution.py:63
  136.5 3.2 %copy-start.1 = (bf16[256,6144]{1,0:T(8,128)(2,1)}, bf16[256,6144]{1,0:T(8,128)(2,1)S(1)}, u32[]{:S(2)}) copy-start(bf16[256,6144]{1,0:T(8,128)(2,1)S(1)} %constant_dynamic-slice_fusion) | copy-start | bytes 9437188
  139.7 5.5 %copy-start = (f32[128,6144]{1,0:T(8,128)S(1)}, f32[128,6144]{1,0:T(8,128)}, u32[]{:S(2)}) copy-start(f32[128,6144]{1,0:T(8,128)} %gather_fusion) | copy-start | bytes 9437188
  139.7 76.5 %all-to-all-start = ((bf16[256,8,768]{0,2,1:T(8,128)(2,1)}), bf16[256,8,768]{0,2,1:T(8,128)(2,1)}, u32[]{:S(2)}, u32[]{:S(2)}) async-start(bf16[256,8,768]{0,2,1:T(8,128)(2,1)} %bitcast.41), calls=%async_computation.1 | async-start | bytes 6291456 | tf_op jit(solution)/shard_map/all_to_all | solution.py:71
Sparse Core Ops, SparseCore 0:
  23.5 46.6 reduce-scatter.1
Sparse Core Ops, SparseCore 1:
  25.5 84.6 all-gather.1
